TPU v7x, 256 devices: a whole 4x4x8 slice. The times are simulated.
256 devices in a mesh: row: 16 (over y, x), col: 16 (over z, core).
Axes of the slice: x: 4, y: 4, z: 8, core: 2. Of those that a mesh axis runs over, the one named last changes fastest.
Arguments:
- block_values: float32 [16, 16, 40, 128, 128], P('row', 'col'), may hold values from 7.8125e-06 to 0.00078125
- block_index: int32 [16, 16, 2, 40], P('row', 'col'), may hold values from 0 to 31, as said below
- block_count: int32 [16, 16], P('row', 'col'), may hold values from 1 to 40, as said below
- strength: float32 [32], replicated, may hold values from 1 to 30
- raw_scores: float32 [512, 32, 128], P(('row', 'col')), may hold values from -24 to 24
Outputs:
- smoothed: float32 [512, 32, 128], P(('row', 'col'))
- final_residual: float32 [512, 32, 128], P(('row', 'col'))
Inputs may be any that keep to these rules, and one draw needn't show every extreme that they name: `block_count`: some device has exactly 40 live slots; the others hold between half and all of their share of the upper triangle, scaled to 40. `block_index`: the live slots of one device name distinct blocks, each with global block row at most its global block column; slots at or above the count hold pairs in range that are ignored.
All inputs are finite; a program needn't handle non-finite values.
Results may differ from a plain program's by a relative error of at most 0.0003.
Values sent between devices are 32-bit elements; how exact they have to be, the bound alone decides.
A program may use at most 64 MiB of HBM per device.

v0:
```python
import jax
import jax.numpy as jnp
from jax import lax
from jax.sharding import PartitionSpec as P

ITERS = 3


def local_terms(values, row_index, col_index, panel_rows, panel_cols):
    picked_cols = jnp.take(panel_cols, col_index, axis=0)
    picked_rows = jnp.take(panel_rows, row_index, axis=0)
    to_rows = jnp.einsum("crk,cik->cri", picked_cols, values, precision=lax.Precision.HIGHEST)
    to_cols = jnp.einsum("cri,cik->crk", picked_rows, values, precision=lax.Precision.HIGHEST)
    row_part = jax.ops.segment_sum(to_rows, row_index, num_segments=panel_rows.shape[0])
    col_part = jax.ops.segment_sum(to_cols, col_index, num_segments=panel_cols.shape[0])
    return (row_part, col_part)


def fold_terms(row_part, col_part):
    return lax.psum_scatter(row_part, "col", scatter_dimension=0, tiled=True) + lax.psum_scatter(
        col_part, "row", scatter_dimension=0, tiled=True
    )


def total(field):
    return jnp.sum(field, axis=(0, 2))


def global_sum(partial_sum):
    return lax.psum(partial_sum, ("row", "col"))


def shards(block_values, block_index, block_count, strength, raw_scores):
    values = block_values[0, 0]
    row_index = block_index[0, 0, 0]
    col_index = block_index[0, 0, 1]
    live_mask = (jnp.arange(values.shape[0], dtype=jnp.int32) < block_count[0, 0]).astype(
        jnp.float32
    )
    masked = values * live_mask[:, None, None]
    segment = raw_scores.shape[0]
    block_size = raw_scores.shape[2]
    rows_here = lax.axis_size("col") * segment
    cols_here = lax.axis_size("row") * segment
    ones_rows = jnp.ones((rows_here, 1, block_size), jnp.float32)
    ones_cols = jnp.ones((cols_here, 1, block_size), jnp.float32)
    degree_rows, degree_cols = local_terms(masked, row_index, col_index, ones_rows, ones_cols)
    degree = fold_terms(degree_rows, degree_cols)
    gains = strength[None, :, None]
    smoothed = jnp.zeros_like(raw_scores)
    residual = raw_scores
    direction = raw_scores
    norm_now = global_sum(total(residual * residual))
    for iteration in range(ITERS):
        panel_rows = lax.all_gather(direction, "col", axis=0, tiled=True)
        panel_cols = lax.all_gather(direction, "row", axis=0, tiled=True)
        row_part, col_part = local_terms(masked, row_index, col_index, panel_rows, panel_cols)
        product = fold_terms(row_part, col_part)
        image = direction + gains * (degree * direction - product)
        step_size = norm_now / global_sum(total(direction * image))
        smoothed = smoothed + step_size[None, :, None] * direction
        residual = residual - step_size[None, :, None] * image
        norm_next = global_sum(total(residual * residual))
        direction = residual + (norm_next / norm_now)[None, :, None] * direction
        norm_now = norm_next
    return (smoothed, residual)


def solution(mesh):
    placed = (
        P("row", "col", None, None, None),
        P("row", "col", None, None),
        P("row", "col"),
        P(),
        P(("row", "col"), None, None),
    )
    return jax.shard_map(
        shards,
        mesh=mesh,
        in_specs=placed,
        out_specs=(P(("row", "col"), None, None), P(("row", "col"), None, None)),
        check_vma=False,
    )
```

profile of v0, /device:TPU:1, one launch (start us, length us, event | category | flops | bytes accessed | tf_op | source)
XLA Modules:
  0.0 916.9 jit_solution(5695150841030016190)
XLA Ops:
  9.4 23.0 %all_gather.19 = f32[32,32,128]{2,1,0:T(8,128)S(1)} all-gather(f32[2,32,128]{2,1,0:T(8,128)} %param.13), channel_id=1, replica_groups=mesh['row'=16,'col'=16] {'col'}, dimensions={0}, use_global_device_ids=true | all-gather | bytes 557056 | tf_op jit(solution)/shard_map/all_gather | solution.py:55
  33.0 5.0 fusion.4
  38.1 4.9 scatter_fusion.1
  43.0 0.8 copy-done.3
  43.9 19.6 %all_gather.18 = f32[32,32,128]{2,1,0:T(8,128)S(1)} all-gather(f32[2,32,128]{2,1,0:T(8,128)S(1)} %copy-done.7), channel_id=1, replica_groups=mesh['row'=16,'col'=16] {'row'}, dimensions={0}, use_global_device_ids=true | all-gather | bytes 557056 | tf_op jit(solution)/shard_map/all_gather | solution.py:56
  63.4 1.4 gather_fusion.2
  64.9 6.2 fusion.5
  71.1 4.7 scatter_fusion
  75.8 0.8 copy-done.4
  80.5 4.3 fusion.7
  84.7 0.9 scatter_custom_fusion
  85.7 2.3 fusion.6
  88.7 58.4 %all-reduce.1 = f32[32,1,128]{2,0,1:T(8,128)S(1)} all-reduce(f32[32,1,128]{2,0,1:T(8,128)S(1)} %bitcast.49), channel_id=3, replica_groups=mesh['row'=16,'col'=16] {'row'}, use_global_device_ids=true, to_apply=%region_5.7.clone | all-reduce | flops 4096 | bytes 32768
  147.1 61.3 %all-reduce = f32[32,1,128]{2,0,1:T(8,128)S(1)} all-reduce(f32[32,1,128]{2,0,1:T(8,128)S(1)} %bitcast.48), channel_id=2, replica_groups=mesh['row'=16,'col'=16] {'col'}, use_global_device_ids=true, to_apply=%region_3.5.clone | all-reduce | flops 4096 | bytes 32768
  208.5 1.0 multiply_reduce_fusion.4
  209.5 74.0 %all-reduce.2 = (f32[32]{0:T(128)S(1)}, f32[32]{0:T(128)S(1)}) all-reduce(f32[32]{0:T(128)S(1)} %get-tuple-element.5, f32[32]{0:T(128)S(1)} %get-tuple-element.4), channel_id=1, replica_groups=mesh['row'=16,'col'=16] {'row','col'}, use_global_device_ids=true, to_apply=%region_1.2 | all-reduce | flops 64 | bytes 512 | tf_op jit(solution)/shard_map/psum | solution.py:30
  283.5 1.0 multiply_reduce_fusion.3
  284.5 74.5 %psum.44 = f32[32]{0:T(128)S(1)} all-reduce(f32[32]{0:T(128)S(1)} %get-tuple-element.10), channel_id=1, replica_groups=mesh['row'=16,'col'=16] {'row','col'}, use_global_device_ids=true, to_apply=%region_13.16 | all-reduce | flops 32 | bytes 256 | tf_op jit(solution)/shard_map/psum | solution.py:30
  359.0 17.2 %all_gather.21 = f32[32,32,128]{2,1,0:T(8,128)S(1)} all-gather(f32[2,32,128]{2,1,0:T(8,128)S(1)} %multiply_add_fusion.4), channel_id=1, replica_groups=mesh['row'=16,'col'=16] {'col'}, dimensions={0}, use_global_device_ids=true | all-gather | bytes 557056 | tf_op jit(solution)/shard_map/all_gather | solution.py:55
  376.2 1.4 gather_fusion.5
  377.7 4.3 fusion.2
  382.1 4.7 scatter_fusion.3
  386.8 0.8 copy-done.5
  387.7 19.2 %all_gather.20 = f32[32,32,128]{2,1,0:T(8,128)S(1)} all-gather(f32[2,32,128]{2,1,0:T(8,128)S(1)} %multiply_add_fusion.4), channel_id=1, replica_groups=mesh['row'=16,'col'=16] {'row'}, dimensions={0}, use_global_device_ids=true | all-gather | bytes 557056 | tf_op jit(solution)/shard_map/all_gather | solution.py:56
  406.8 1.4 gather_fusion.4
  408.3 6.2 fusion.3
  414.5 4.7 scatter_fusion.2
  419.2 0.8 copy-done.6
  420.1 38.4 %reduce-scatter.15.cloned.1.call-done = f32[2,32,128]{2,1,0:T(8,128)} async-done(((f32[32,32,128]{2,1,0:T(8,128)}), f32[2,32,128]{2,1,0:T(8,128)}) %reduce-scatter.15.cloned.1.call-update) | async-done | bytes 32784 | tf_op jit(solution)/shard_map/reduce_scatter | solution.py:20
  458.5 57.2 %reduce-scatter.13.cloned.1.call-done = f32[2,32,128]{2,1,0:T(8,128)} async-done(((f32[32,32,128]{2,1,0:T(8,128)}), f32[2,32,128]{2,1,0:T(8,128)}) %reduce-scatter.13.cloned.1.call-update) | async-done | bytes 32784 | tf_op jit(solution)/shard_map/reduce_scatter | solution.py:20
  515.7 1.0 multiply_reduce_fusion.2
  516.7 79.6 %psum.45 = f32[32]{0:T(128)S(1)} all-reduce(f32[32]{0:T(128)S(1)} %multiply_reduce_fusion.2), channel_id=1, replica_groups=mesh['row'=16,'col'=16] {'row','col'}, use_global_device_ids=true, to_apply=%region_19.22 | all-reduce | flops 32 | bytes 256 | tf_op jit(solution)/shard_map/psum | solution.py:30
  596.2 1.0 multiply_reduce_fusion.1
  597.2 72.4 %psum.46 = f32[32]{0:T(128)S(1)} all-reduce(f32[32]{0:T(128)S(1)} %get-tuple-element.8), channel_id=1, replica_groups=mesh['row'=16,'col'=16] {'row','col'}, use_global_device_ids=true, to_apply=%region_21.24 | all-reduce | flops 32 | bytes 256 | tf_op jit(solution)/shard_map/psum | solution.py:30
  669.6 18.1 %all_gather.23 = f32[32,32,128]{2,1,0:T(8,128)S(1)} all-gather(f32[2,32,128]{2,1,0:T(8,128)S(1)} %multiply_add_fusion.2), channel_id=1, replica_groups=mesh['row'=16,'col'=16] {'col'}, dimensions={0}, use_global_device_ids=true | all-gather | bytes 557056 | tf_op jit(solution)/shard_map/all_gather | solution.py:55
  687.7 1.4 gather_fusion.7
  689.2 4.3 fusion
  693.6 4.7 scatter_fusion.5
  698.3 0.8 copy-done.2
  699.1 19.2 %all_gather.22 = f32[32,32,128]{2,1,0:T(8,128)S(1)} all-gather(f32[2,32,128]{2,1,0:T(8,128)S(1)} %multiply_add_fusion.2), channel_id=1, replica_groups=mesh['row'=16,'col'=16] {'row'}, dimensions={0}, use_global_device_ids=true | all-gather | bytes 557056 | tf_op jit(solution)/shard_map/all_gather | solution.py:56
  718.4 1.4 gather_fusion.6
  719.8 5.3 fusion.1
  725.2 2.7 scatter_fusion.4
  728.7 41.8 %reduce-scatter.19.cloned.1.call-done = f32[2,32,128]{2,1,0:T(8,128)} async-done(((f32[32,32,128]{2,1,0:T(8,128)}), f32[2,32,128]{2,1,0:T(8,128)}) %reduce-scatter.19.cloned.1.call-update) | async-done | bytes 32784 | tf_op jit(solution)/shard_map/reduce_scatter | solution.py:20
  770.5 57.3 %reduce-scatter.17.cloned.1.call-done = f32[2,32,128]{2,1,0:T(8,128)} async-done(((f32[32,32,128]{2,1,0:T(8,128)}), f32[2,32,128]{2,1,0:T(8,128)}) %reduce-scatter.17.cloned.1.call-update) | async-done | bytes 32784 | tf_op jit(solution)/shard_map/reduce_scatter | solution.py:20
  827.8 1.0 multiply_reduce_fusion
  828.8 79.8 %psum.47 = f32[32]{0:T(128)S(1)} all-reduce(f32[32]{0:T(128)S(1)} %multiply_reduce_fusion), channel_id=1, replica_groups=mesh['row'=16,'col'=16] {'row','col'}, use_global_device_ids=true, to_apply=%region_27.30 | all-reduce | flops 32 | bytes 256 | tf_op jit(solution)/shard_map/psum | solution.py:30
  908.5 1.5 multiply_subtract_fusion
  (58 shorter events, 6.9 us)
Async XLA Ops:
  7.2 201.3 %reduce-scatter.11.cloned.1.call-start = ((), (), s32[]{:S(2)}) async-start(), calls=%async_computation.7 | async-start | bytes 557056 | tf_op jit(solution)/shard_map/reduce_scatter | solution.py:20
  33.0 10.9 %copy-start.7 = (f32[2,32,128]{2,1,0:T(8,128)S(1)}, f32[2,32,128]{2,1,0:T(8,128)}, u32[]{:S(2)}) copy-start(f32[2,32,128]{2,1,0:T(8,128)} %param.13) | copy-start | bytes 98308
  38.0 26.9 %copy-start = (f32[1,1,40,128,128]{4,3,2,1,0:T(8,128)S(1)}, f32[1,1,40,128,128]{4,3,2,1,0:T(8,128)}, u32[]{:S(2)}) copy-start(f32[1,1,40,128,128]{4,3,2,1,0:T(8,128)} %param.9) | copy-start | bytes 7864324
  42.9 0.8 copy-start.3
  43.8 164.7 %reduce-scatter.9.cloned.1.call-start = ((), (), s32[]{:S(2)}) async-start(), calls=%async_computation.6 | async-start | bytes 557056 | tf_op jit(solution)/shard_map/reduce_scatter | solution.py:20
  71.1 6.8 copy-start.10
  71.1 7.4 copy-start.9
  75.8 0.8 copy-start.4
  76.7 381.8 %reduce-scatter.15.cloned.1.call-start = ((), (), s32[]{:S(2)}) async-start(), calls=%async_computation.9 | async-start | bytes 557056 | tf_op jit(solution)/shard_map/reduce_scatter | solution.py:20
  80.4 128.1 %copy-start.8 = (f32[32]{0:T(128)S(1)}, f32[32]{0:T(128)}, u32[]{:S(2)}) copy-start(f32[32]{0:T(128)} %param.12) | copy-start | bytes 388
  386.8 0.8 copy-start.5
  387.6 128.1 %reduce-scatter.13.cloned.1.call-start = ((), (), s32[]{:S(2)}) async-start(), calls=%async_computation.8 | async-start | bytes 557056 | tf_op jit(solution)/shard_map/reduce_scatter | solution.py:20
  419.2 0.8 copy-start.6
  420.0 350.5 %reduce-scatter.19.cloned.1.call-start = ((), (), s32[]{:S(2)}) async-start(), calls=%async_computation.11 | async-start | bytes 557056 | tf_op jit(solution)/shard_map/reduce_scatter | solution.py:20
  698.3 0.8 copy-start.2
  699.1 128.7 %reduce-scatter.17.cloned.1.call-start = ((), (), s32[]{:S(2)}) async-start(), calls=%async_computation.10 | async-start | bytes 557056 | tf_op jit(solution)/shard_map/reduce_scatter | solution.py:20
  727.9 0.8 copy-start.1
Sparse Core Ops, SparseCore 0:
  43.9 73.4 reduce-scatter.10
  120.0 55.2 reduce-scatter.8
  387.7 70.6 reduce-scatter.14
  461.0 54.6 reduce-scatter.12
  699.2 71.2 reduce-scatter.18
  773.0 54.7 reduce-scatter.16
where the time goes:
time: 918 us; the launch traced here: 917 us
  blocking collectives  616 us (67%)
  waiting for transfers between devices  195 us (21%)
  matrix products  37.9 us (4%)
  other arithmetic  35.4 us (4%)
  between operations  16.3 us (2%)
  local copies, waits for them, and re-layouts  15.9 us (2%)
    psum x5, blocking collectives, global_sum(): return lax.psum(partial_sum, ('row', 'col'))  380 us
    unnamed x2, blocking collectives  120 us
    reduce_scatter x3, waiting for transfers between devices, fold_terms(): lax.psum_scatter(row_part, 'col', scatter_dimension=0, tiled=True)  115 us
    reduce_scatter x3, waiting for transfers between devices, fold_terms(): lax.psum_scatter(col_part, 'row', scatter_dimension=0, tiled=True)  80.2 us
    all_gather x3, blocking collectives, shards(): panel_rows = lax.all_gather(direction, 'col', axis=0, tiled=True)  58.3 us
    all_gather x3, blocking collectives, shards(): panel_cols = lax.all_gather(direction, 'row', axis=0, tiled=True)  58 us
    dot_general x4, matrix products, local_terms(): jnp.einsum('crk,cik->cri', picked_cols, values, precision=lax.Precision.H...  22 us
  transfers between devices with their start and end apart: 6, of which 4 were waited for; matrix products, arithmetic and copies ran while one was open for 5% of the time, Pallas kernels for 0%

commit v1 on v0

--- a/solution.py
+++ b/solution.py
@@ -1,9 +1,39 @@
+import functools
 import jax
 import jax.numpy as jnp
 from jax import lax
 from jax.sharding import PartitionSpec as P
 
 ITERS = 3
+
+
+def review_group(xin, ndim_at):
+    xin = jnp.moveaxis(xin, 0, ndim_at)
+    u1 = xin.shape
+    return xin.reshape(*u1[:ndim_at], u1[ndim_at] * u1[ndim_at + 1], *u1[ndim_at + 2 :])
+
+
+def place_the_turns(arr, net_axis, out_dim):
+    width = jax.lax.axis_size(net_axis)
+    local_now = map(lambda i: (i, (i + 1) % width), range(width))
+    rack = list(local_now)
+    chunks = [(b, p) for p, b in rack]
+    z1, block_last = ([], [])
+    for h in tuple(range(width - 1)):
+        if h % 2 == 0:
+            z1.append(jax.lax.ppermute(z1[-1] if z1 else arr, axis_name=net_axis, perm=rack))
+        else:
+            new = jax.lax.ppermute(block_last[-1] if block_last else arr, net_axis, chunks)
+            block_last.append(new)
+    k_now = jnp.stack([*z1[::-1], arr, *block_last])
+    e_now = jax.lax.axis_index(net_axis)
+    current_arr = len(z1)
+    side_arr = e_now - current_arr
+    k_now = k_now[(jnp.arange(width) - side_arr) % width]
+    return review_group(k_now, out_dim)
+
+
+compute_members_all = functools.partial(place_the_turns, net_axis="row", out_dim=0)
 
 
 def local_terms(values, row_index, col_index, panel_rows, panel_cols):
@@ -53,7 +83,7 @@
     norm_now = global_sum(total(residual * residual))
     for iteration in range(ITERS):
         panel_rows = lax.all_gather(direction, "col", axis=0, tiled=True)
-        panel_cols = lax.all_gather(direction, "row", axis=0, tiled=True)
+        panel_cols = compute_members_all(direction)
         row_part, col_part = local_terms(masked, row_index, col_index, panel_rows, panel_cols)
         product = fold_terms(row_part, col_part)
         image = direction + gains * (degree * direction - product)

time: 918 us -> 1070 us (1.17); the launches traced: 917 us -> 1060 us
  starting transfers between devices: 0.25 us -> 106 us
  blocking collectives: 616 us -> 571 us
  local copies, waits for them, and re-layouts: 15.9 us -> 59.7 us
  waiting for transfers between devices: 195 us -> 230 us
    ppermute x0 -> x45, starting transfers between devices: none -> 106 us  [the longest x21 101 us: place_the_turns(): jax.lax.ppermute(block_last[-1] if block_last else arr, net_axis, chunks)]
    all_gather x3 -> x0, blocking collectives: 58 us -> none  [shards(): panel_cols = lax.all_gather(direction, 'row', axis=0, tiled=True)]
    unnamed x24 -> x107, local copies, waits for them, and re-layouts: 5.96 us -> 43 us
    ppermute x0 -> x45, waiting for transfers between devices: none -> 32.7 us  [the longest x24 30.1 us: place_the_turns(): jax.lax.ppermute(z1[-1] if z1 else arr, axis_name=net_axis, perm=rack)]
    all_gather x3, blocking collectives: 58.3 us -> 71.6 us  [shards(): panel_rows = lax.all_gather(direction, 'col', axis=0, tiled=True)]
  transfers between devices with their start and end apart: 6 -> 51, of which waited for: 4 -> 23; matrix products, arithmetic and copies ran while one was open for 5% -> 11% of each run, Pallas kernels for 0% -> 0%
where the time goes in v1:
time: 1070 us; the launch traced here: 1060 us
  blocking collectives  571 us (53%)
  waiting for transfers between devices  230 us (21%)
  starting transfers between devices  106 us (10%)
  local copies, waits for them, and re-layouts  59.7 us (6%)
  matrix products  38 us (4%)
  other arithmetic  35.9 us (3%)
  between operations  17.1 us (2%)
    psum x5, blocking collectives, global_sum(): return lax.psum(partial_sum, ('row', 'col'))  381 us
    unnamed x2, blocking collectives  119 us
    reduce_scatter x3, waiting for transfers between devices, fold_terms(): lax.psum_scatter(row_part, 'col', scatter_dimension=0, tiled=True)  114 us
    ppermute x21, starting transfers between devices, place_the_turns(): jax.lax.ppermute(block_last[-1] if block_last else arr, net_axis, chunks)  101 us
    reduce_scatter x3, waiting for transfers between devices, fold_terms(): lax.psum_scatter(col_part, 'row', scatter_dimension=0, tiled=True)  83.1 us
    all_gather x3, blocking collectives, shards(): panel_rows = lax.all_gather(direction, 'col', axis=0, tiled=True)  71.6 us
    unnamed x107, local copies, waits for them, and re-layouts  43 us
    ppermute x24, waiting for transfers between devices, place_the_turns(): jax.lax.ppermute(z1[-1] if z1 else arr, axis_name=net_axis, perm=rack)  30.1 us
  transfers between devices with their start and end apart: 51, of which 23 were waited for; matrix products, arithmetic and copies ran while one was open for 11% of the time, Pallas kernels for 0%

profile of v1, /device:TPU:1, one launch (start us, length us, event | category | flops | bytes accessed | tf_op | source)
XLA Modules:
  0.0 1057.9 jit_solution(17116977009839217490)
XLA Ops:
  13.1 22.5 %all_gather.9 = f32[32,32,128]{2,1,0:T(8,128)S(1)} all-gather(f32[2,32,128]{2,1,0:T(8,128)} %param.13), channel_id=1, replica_groups=mesh['row'=16,'col'=16] {'col'}, dimensions={0}, use_global_device_ids=true | all-gather | bytes 557056 | tf_op jit(solution)/shard_map/all_gather | solution.py:85
  37.2 5.4 collective-permute-done.1
  43.2 4.9 collective-permute-start.9
  48.6 5.0 fusion.4
  53.6 4.8 collective-permute-start.10
  58.5 4.9 scatter_fusion.1
  64.3 4.8 collective-permute-start.11
  70.2 5.1 collective-permute-start.12
  76.3 5.1 collective-permute-start.13
  82.4 5.1 collective-permute-start.14
  100.6 6.2 fusion.5
  106.8 4.7 scatter_fusion
  124.8 55.8 %all-reduce.1 = f32[32,1,128]{2,0,1:T(8,128)S(1)} all-reduce(f32[32,1,128]{2,0,1:T(8,128)S(1)} %bitcast.153), channel_id=3, replica_groups=mesh['row'=16,'col'=16] {'row'}, use_global_device_ids=true, to_apply=%region_5.7.clone | all-reduce | flops 4096 | bytes 32768
  180.6 63.0 %all-reduce = f32[32,1,128]{2,0,1:T(8,128)S(1)} all-reduce(f32[32,1,128]{2,0,1:T(8,128)S(1)} %bitcast.152), channel_id=2, replica_groups=mesh['row'=16,'col'=16] {'col'}, use_global_device_ids=true, to_apply=%region_3.5.clone | all-reduce | flops 4096 | bytes 32768
  244.6 74.0 %all-reduce.2 = (f32[32]{0:T(128)S(1)}, f32[32]{0:T(128)S(1)}) all-reduce(f32[32]{0:T(128)S(1)} %get-tuple-element.5, f32[32]{0:T(128)S(1)} %get-tuple-element.4), channel_id=1, replica_groups=mesh['row'=16,'col'=16] {'row','col'}, use_global_device_ids=true, to_apply=%region_1.2 | all-reduce | flops 64 | bytes 512 | tf_op jit(solution)/shard_map/psum | solution.py:60
  319.6 74.4 %psum.44 = f32[32]{0:T(128)S(1)} all-reduce(f32[32]{0:T(128)S(1)} %get-tuple-element.10), channel_id=1, replica_groups=mesh['row'=16,'col'=16] {'row','col'}, use_global_device_ids=true, to_apply=%region_13.16 | all-reduce | flops 32 | bytes 256 | tf_op jit(solution)/shard_map/psum | solution.py:60
  395.8 5.0 collective-permute-done.15
  400.8 4.8 collective-permute-start.23
  406.9 4.8 collective-permute-start.24
  412.9 4.8 collective-permute-start.25
  419.0 4.8 collective-permute-start.26
  425.3 4.8 collective-permute-start.27
  431.5 24.1 %all_gather.10 = f32[32,32,128]{2,1,0:T(8,128)S(1)} all-gather(f32[2,32,128]{2,1,0:T(8,128)S(1)} %multiply_add_fusion.4), channel_id=1, replica_groups=mesh['row'=16,'col'=16] {'col'}, dimensions={0}, use_global_device_ids=true | all-gather | bytes 557056 | tf_op jit(solution)/shard_map/all_gather | solution.py:85
  457.1 5.1 collective-permute-start.28
  462.2 4.3 fusion.2
  466.6 4.8 scatter_fusion.3
  472.3 4.9 collective-permute-start.29
  494.1 6.2 fusion.3
  500.3 4.7 scatter_fusion.2
  505.9 39.9 %reduce-scatter.15.cloned.1.call-done = f32[2,32,128]{2,1,0:T(8,128)} async-done(((f32[32,32,128]{2,1,0:T(8,128)}), f32[2,32,128]{2,1,0:T(8,128)}) %reduce-scatter.15.cloned.1.call-update) | async-done | bytes 32784 | tf_op jit(solution)/shard_map/reduce_scatter | solution.py:50
  545.8 57.2 %reduce-scatter.13.cloned.1.call-done = f32[2,32,128]{2,1,0:T(8,128)} async-done(((f32[32,32,128]{2,1,0:T(8,128)}), f32[2,32,128]{2,1,0:T(8,128)}) %reduce-scatter.13.cloned.1.call-update) | async-done | bytes 32784 | tf_op jit(solution)/shard_map/reduce_scatter | solution.py:50
  604.0 80.0 %psum.45 = f32[32]{0:T(128)S(1)} all-reduce(f32[32]{0:T(128)S(1)} %multiply_reduce_fusion.2), channel_id=1, replica_groups=mesh['row'=16,'col'=16] {'row','col'}, use_global_device_ids=true, to_apply=%region_19.22 | all-reduce | flops 32 | bytes 256 | tf_op jit(solution)/shard_map/psum | solution.py:60
  684.9 72.3 %psum.46 = f32[32]{0:T(128)S(1)} all-reduce(f32[32]{0:T(128)S(1)} %get-tuple-element.8), channel_id=1, replica_groups=mesh['row'=16,'col'=16] {'row','col'}, use_global_device_ids=true, to_apply=%region_21.24 | all-reduce | flops 32 | bytes 256 | tf_op jit(solution)/shard_map/psum | solution.py:60
  758.5 5.5 collective-permute-done.30
  764.0 4.8 collective-permute-start.38
  770.1 4.8 collective-permute-start.39
  776.1 4.8 collective-permute-start.40
  782.2 4.8 collective-permute-start.41
  788.3 4.8 collective-permute-start.42
  794.5 25.0 %all_gather.11 = f32[32,32,128]{2,1,0:T(8,128)S(1)} all-gather(f32[2,32,128]{2,1,0:T(8,128)S(1)} %multiply_add_fusion.2), channel_id=1, replica_groups=mesh['row'=16,'col'=16] {'col'}, dimensions={0}, use_global_device_ids=true | all-gather | bytes 557056 | tf_op jit(solution)/shard_map/all_gather | solution.py:85
  821.1 5.1 collective-permute-start.43
  826.4 4.3 fusion
  830.8 4.8 scatter_fusion.5
  836.5 4.8 collective-permute-start.44
  859.1 5.3 fusion.1
  867.9 43.2 %reduce-scatter.19.cloned.1.call-done = f32[2,32,128]{2,1,0:T(8,128)} async-done(((f32[32,32,128]{2,1,0:T(8,128)}), f32[2,32,128]{2,1,0:T(8,128)}) %reduce-scatter.19.cloned.1.call-update) | async-done | bytes 32784 | tf_op jit(solution)/shard_map/reduce_scatter | solution.py:50
  911.1 57.1 %reduce-scatter.17.cloned.1.call-done = f32[2,32,128]{2,1,0:T(8,128)} async-done(((f32[32,32,128]{2,1,0:T(8,128)}), f32[2,32,128]{2,1,0:T(8,128)}) %reduce-scatter.17.cloned.1.call-update) | async-done | bytes 32784 | tf_op jit(solution)/shard_map/reduce_scatter | solution.py:50
  969.1 79.9 %psum.47 = f32[32]{0:T(128)S(1)} all-reduce(f32[32]{0:T(128)S(1)} %multiply_reduce_fusion), channel_id=1, replica_groups=mesh['row'=16,'col'=16] {'row','col'}, use_global_device_ids=true, to_apply=%region_27.30 | all-reduce | flops 32 | bytes 256 | tf_op jit(solution)/shard_map/psum | solution.py:60
  (236 shorter events, 103.8 us)
Async XLA Ops:
  7.2 236.5 %reduce-scatter.11.cloned.1.call-start = ((), (), s32[]{:S(2)}) async-start(), calls=%async_computation.7 | async-start | bytes 557056 | tf_op jit(solution)/shard_map/reduce_scatter | solution.py:50
  7.2 29.2 %collective-permute-start = (f32[2,32,128]{2,1,0:T(8,128)}, f32[2,32,128]{2,1,0:T(8,128)S(1)}, u32[]{:S(2)}, u32[]{:S(2)}) collective-permute-start(f32[2,32,128]{2,1,0:T(8,128)} %param.13), channel_id=1, source_target_pairs={{0,16},{16,32},{32,48},{48,64},{64,80},{80,96},{96,112},{112,128},... | collective-permute-start | bytes 98312 | tf_op jit(solution)/shard_map/ppermute | solution.py:24
  9.3 33.8 %collective-permute-start.8 = (f32[2,32,128]{2,1,0:T(8,128)}, f32[2,32,128]{2,1,0:T(8,128)S(1)}, u32[]{:S(2)}, u32[]{:S(2)}) collective-permute-start(f32[2,32,128]{2,1,0:T(8,128)} %param.13), channel_id=1, source_target_pairs={{16,0},{32,16},{48,32},{64,48},{80,64},{96,80},{112,96},{128,112},... | collective-permute-start | bytes 98312 | tf_op jit(solution)/shard_map/ppermute | solution.py:26
  36.4 6.2 collective-permute-start.1
  42.5 6.1 collective-permute-start.2
  43.2 10.5 collective-permute-start.9
  48.6 9.8 collective-permute-start.3
  53.6 10.7 %collective-permute-start.10 = (f32[2,32,128]{2,1,0:T(8,128)S(1)}, f32[2,32,128]{2,1,0:T(8,128)S(1)}, u32[]{:S(2)}, u32[]{:S(2)}) collective-permute-start(f32[2,32,128]{2,1,0:T(8,128)S(1)} %collective-permute-done.9), channel_id=1, source_target_pairs={{16,0},{32,16},{48,32},{64,48},{80,64},{96,80},{112,96},{128,112},... | collective-permute-start | bytes 98312 | tf_op jit(solution)/shard_map/ppermute | solution.py:26
  58.4 10.8 %collective-permute-start.4 = (f32[2,32,128]{2,1,0:T(8,128)S(1)}, f32[2,32,128]{2,1,0:T(8,128)S(1)}, u32[]{:S(2)}, u32[]{:S(2)}) collective-permute-start(f32[2,32,128]{2,1,0:T(8,128)S(1)} %collective-permute-done.3), channel_id=1, source_target_pairs={{0,16},{16,32},{32,48},{48,64},{64,80},{80,96},{96,112},{112,128},... | collective-permute-start | bytes 98312 | tf_op jit(solution)/shard_map/ppermute | solution.py:24
  64.3 179.4 %reduce-scatter.9.cloned.1.call-start = ((), (), s32[]{:S(2)}) async-start(), calls=%async_computation.6 | async-start | bytes 557056 | tf_op jit(solution)/shard_map/reduce_scatter | solution.py:50
  69.2 6.1 collective-permute-start.5
  70.2 6.1 collective-permute-start.12
  75.3 6.3 collective-permute-start.6
  76.3 6.1 collective-permute-start.13
  81.6 6.1 collective-permute-start.7
  82.4 14.5 %collective-permute-start.14 = (f32[2,32,128]{2,1,0:T(8,128)S(1)}, f32[2,32,128]{2,1,0:T(8,128)S(1)}, u32[]{:S(2)}, u32[]{:S(2)}) collective-permute-start(f32[2,32,128]{2,1,0:T(8,128)S(1)} %collective-permute-done.13), channel_id=1, source_target_pairs={{16,0},{32,16},{48,32},{64,48},{80,64},{96,80},{112,96},{128,112},... | collective-permute-start | bytes 98312 | tf_op jit(solution)/shard_map/ppermute | solution.py:26
  112.3 433.5 %reduce-scatter.15.cloned.1.call-start = ((), (), s32[]{:S(2)}) async-start(), calls=%async_computation.9 | async-start | bytes 557056 | tf_op jit(solution)/shard_map/reduce_scatter | solution.py:50
  394.7 6.1 collective-permute-start.15
  400.8 6.1 collective-permute-start.16
  400.8 6.1 collective-permute-start.23
  406.8 6.1 collective-permute-start.17
  406.9 6.1 collective-permute-start.24
  412.9 6.1 collective-permute-start.18
  412.9 6.1 collective-permute-start.25
  419.0 6.1 collective-permute-start.19
  419.0 6.2 collective-permute-start.26
  425.1 6.3 collective-permute-start.20
  425.3 31.8 %collective-permute-start.27 = (f32[2,32,128]{2,1,0:T(8,128)S(1)}, f32[2,32,128]{2,1,0:T(8,128)S(1)}, u32[]{:S(2)}, u32[]{:S(2)}) collective-permute-start(f32[2,32,128]{2,1,0:T(8,128)S(1)} %collective-permute-done.26), channel_id=1, source_target_pairs={{16,0},{32,16},{48,32},{64,48},{80,64},{96,80},{112,96},{128,112},... | collective-permute-start | bytes 98312 | tf_op jit(solution)/shard_map/ppermute | solution.py:26
  431.4 30.7 %collective-permute-start.21 = (f32[2,32,128]{2,1,0:T(8,128)}, f32[2,32,128]{2,1,0:T(8,128)}, u32[]{:S(2)}, u32[]{:S(2)}) collective-permute-start(f32[2,32,128]{2,1,0:T(8,128)} %collective-permute-done.20), channel_id=1, source_target_pairs={{0,16},{16,32},{32,48},{48,64},{64,80},{80,96},{96,112},{112,128},... | collective-permute-start | bytes 98312 | tf_op jit(solution)/shard_map/ppermute | solution.py:24
  457.1 15.2 %collective-permute-start.28 = (f32[2,32,128]{2,1,0:T(8,128)S(1)}, f32[2,32,128]{2,1,0:T(8,128)}, u32[]{:S(2)}, u32[]{:S(2)}) collective-permute-start(f32[2,32,128]{2,1,0:T(8,128)S(1)} %collective-permute-done.27), channel_id=1, source_target_pairs={{16,0},{32,16},{48,32},{64,48},{80,64},{96,80},{112,96},{128,112},... | collective-permute-start | bytes 98312 | tf_op jit(solution)/shard_map/ppermute | solution.py:26
  462.2 15.0 %collective-permute-start.22 = (f32[2,32,128]{2,1,0:T(8,128)}, f32[2,32,128]{2,1,0:T(8,128)}, u32[]{:S(2)}, u32[]{:S(2)}) collective-permute-start(f32[2,32,128]{2,1,0:T(8,128)} %collective-permute-done.21), channel_id=1, source_target_pairs={{0,16},{16,32},{32,48},{48,64},{64,80},{80,96},{96,112},{112,128},... | collective-permute-start | bytes 98312 | tf_op jit(solution)/shard_map/ppermute | solution.py:24
  472.2 130.8 %reduce-scatter.13.cloned.1.call-start = ((), (), s32[]{:S(2)}) async-start(), calls=%async_computation.8 | async-start | bytes 557056 | tf_op jit(solution)/shard_map/reduce_scatter | solution.py:50
  472.3 17.8 %collective-permute-start.29 = (f32[2,32,128]{2,1,0:T(8,128)}, f32[2,32,128]{2,1,0:T(8,128)S(1)}, u32[]{:S(2)}, u32[]{:S(2)}) collective-permute-start(f32[2,32,128]{2,1,0:T(8,128)} %collective-permute-done.28), channel_id=1, source_target_pairs={{16,0},{32,16},{48,32},{64,48},{80,64},{96,80},{112,96},{128,112},... | collective-permute-start | bytes 98312 | tf_op jit(solution)/shard_map/ppermute | solution.py:26
  505.9 405.3 %reduce-scatter.19.cloned.1.call-start = ((), (), s32[]{:S(2)}) async-start(), calls=%async_computation.11 | async-start | bytes 557056 | tf_op jit(solution)/shard_map/reduce_scatter | solution.py:50
  757.9 6.1 collective-permute-start.30
  764.0 6.1 collective-permute-start.31
  764.0 6.1 collective-permute-start.38
  770.1 6.1 collective-permute-start.32
  770.1 6.1 collective-permute-start.39
  776.1 6.1 collective-permute-start.33
  782.2 6.1 collective-permute-start.41
  788.3 6.2 collective-permute-start.35
  788.3 32.8 %collective-permute-start.42 = (f32[2,32,128]{2,1,0:T(8,128)S(1)}, f32[2,32,128]{2,1,0:T(8,128)}, u32[]{:S(2)}, u32[]{:S(2)}) collective-permute-start(f32[2,32,128]{2,1,0:T(8,128)S(1)} %collective-permute-done.41), channel_id=1, source_target_pairs={{16,0},{32,16},{48,32},{64,48},{80,64},{96,80},{112,96},{128,112},... | collective-permute-start | bytes 98312 | tf_op jit(solution)/shard_map/ppermute | solution.py:26
  794.5 31.6 %collective-permute-start.36 = (f32[2,32,128]{2,1,0:T(8,128)}, f32[2,32,128]{2,1,0:T(8,128)}, u32[]{:S(2)}, u32[]{:S(2)}) collective-permute-start(f32[2,32,128]{2,1,0:T(8,128)} %collective-permute-done.35), channel_id=1, source_target_pairs={{0,16},{16,32},{32,48},{48,64},{64,80},{80,96},{96,112},{112,128},... | collective-permute-start | bytes 98312 | tf_op jit(solution)/shard_map/ppermute | solution.py:24
  821.1 15.4 %collective-permute-start.43 = (f32[2,32,128]{2,1,0:T(8,128)}, f32[2,32,128]{2,1,0:T(8,128)}, u32[]{:S(2)}, u32[]{:S(2)}) collective-permute-start(f32[2,32,128]{2,1,0:T(8,128)} %collective-permute-done.42), channel_id=1, source_target_pairs={{16,0},{32,16},{48,32},{64,48},{80,64},{96,80},{112,96},{128,112},... | collective-permute-start | bytes 98312 | tf_op jit(solution)/shard_map/ppermute | solution.py:26
  826.1 15.2 %collective-permute-start.37 = (f32[2,32,128]{2,1,0:T(8,128)}, f32[2,32,128]{2,1,0:T(8,128)}, u32[]{:S(2)}, u32[]{:S(2)}) collective-permute-start(f32[2,32,128]{2,1,0:T(8,128)} %collective-permute-done.36), channel_id=1, source_target_pairs={{0,16},{16,32},{32,48},{48,64},{64,80},{80,96},{96,112},{112,128},... | collective-permute-start | bytes 98312 | tf_op jit(solution)/shard_map/ppermute | solution.py:24
  836.5 131.7 %reduce-scatter.17.cloned.1.call-start = ((), (), s32[]{:S(2)}) async-start(), calls=%async_computation.10 | async-start | bytes 557056 | tf_op jit(solution)/shard_map/reduce_scatter | solution.py:50
  836.5 18.6 %collective-permute-start.44 = (f32[2,32,128]{2,1,0:T(8,128)}, f32[2,32,128]{2,1,0:T(8,128)S(1)}, u32[]{:S(2)}, u32[]{:S(2)}) collective-permute-start(f32[2,32,128]{2,1,0:T(8,128)} %collective-permute-done.43), channel_id=1, source_target_pairs={{16,0},{32,16},{48,32},{64,48},{80,64},{96,80},{112,96},{128,112},... | collective-permute-start | bytes 98312 | tf_op jit(solution)/shard_map/ppermute | solution.py:26
  (33 other events, 1544.6 us)
Sparse Core Ops, SparseCore 0:
  64.4 75.8 reduce-scatter.10
  143.0 55.6 reduce-scatter.8
  472.4 73.4 reduce-scatter.14
  548.4 54.6 reduce-scatter.12
  836.6 74.4 reduce-scatter.18
  913.6 54.5 reduce-scatter.16
